TPU v7x, 256 devices: a whole 4x4x8 slice. The times are simulated.
256 devices in a mesh: dp: 16 (over x_lo, y, core), mp: 8 (over z), side: 2 (over x_hi).
Axes of the slice: x: 4 (x_hi: 2, x_lo: 2; x = x_hi * 2 + x_lo), y: 4, z: 8, core: 2. Of those that a mesh axis runs over, the one named last changes fastest.
Arguments:
- tokens: bfloat16 [4096, 3072], P('dp', 'mp'), may hold values from -6 to 6
- up_weight: bfloat16 [2, 3072, 6144], P('side', 'dp', 'mp'), may hold values from -0.109375 to 0.109375
- down_weight: bfloat16 [2, 6144, 3072], P('side', 'mp', 'dp'), may hold values from -0.078125 to 0.078125
- mod_table: float32 [2, 50, 3, 3072], P('side'), may hold values from -3 to 3
- timesteps: int32 [16], P('dp'), may hold values from 0 to 49
- valid_counts: int32 [16], replicated, may hold values from 64 to 256, as said below
Outputs:
- block_out: bfloat16 [2, 4096, 3072], P('side', 'dp', 'mp')
- up_grads: float32 [3072, 6144], P(('dp', 'side'), 'mp')
- down_grads: float32 [6144, 3072], P('mp', ('dp', 'side'))
Inputs may be any that keep to these rules, and one draw needn't show every extreme that they name: `valid_counts`: every image has at least 64 valid tokens, and in every draw some image has all 256 valid.
All inputs are finite; a program needn't handle non-finite values.
Results may differ from a plain program's by a relative error of at most 0.018.
Values may be sent and summed in bfloat16 or wider, within the bound.
A program may use at most 64 MiB of HBM per device.

v0:
```python
import jax
import jax.numpy as jnp
from jax import lax
from jax.sharding import PartitionSpec as P


def passed_along(x, axis, by):
    peers = lax.axis_size(axis)
    pairs = [(i, i + by) for i in range(peers) if 0 <= i + by < peers]
    return lax.ppermute(x, axis, pairs)


def gelu_tanh(values):
    return jax.nn.gelu(values, approximate=True)


def shards(tokens, up_weight, down_weight, mod_table, timesteps, valid_counts):
    gathered = lax.all_gather(tokens, "mp", axis=1, tiled=True)
    width = gathered.shape[1]
    shard_width = tokens.shape[1]
    mp_offset = lax.axis_index("mp") * shard_width
    is_student = lax.axis_index("side") == 1
    wide = gathered.astype(jnp.float32)
    average = jnp.mean(wide, axis=-1, keepdims=True)
    centred = wide - average
    variance = jnp.mean(centred * centred, axis=-1, keepdims=True)
    scaled = centred * lax.rsqrt(variance + 1e-06)
    plan = mod_table.shape[1]
    one_hot = (jnp.arange(plan, dtype=jnp.int32)[None, :] == timesteps[0]).astype(jnp.float32)
    modulation = jnp.dot(
        one_hot,
        mod_table[0].reshape(plan, 3 * width),
        precision=lax.Precision.HIGHEST,
        preferred_element_type=jnp.float32,
    ).reshape(3, width)
    normed = (scaled * (1.0 + modulation[1]) + modulation[0]).astype(jnp.bfloat16)
    gate_row = modulation[2]
    hidden_pre = jnp.dot(
        normed,
        lax.all_gather(up_weight[0], "dp", axis=0, tiled=True),
        preferred_element_type=jnp.float32,
    )
    hidden_act = gelu_tanh(hidden_pre).astype(jnp.bfloat16)
    down_full = lax.all_gather(down_weight[0], "dp", axis=1, tiled=True)
    partial_value = jnp.dot(hidden_act, down_full, preferred_element_type=jnp.float32)
    positions = jnp.arange(normed.shape[0], dtype=jnp.int32)
    own_count = lax.dynamic_index_in_dim(valid_counts, lax.axis_index("dp"), 0, keepdims=False)
    valid_col = (positions < own_count).astype(jnp.float32)[:, None]
    valid_total = jnp.sum(valid_counts).astype(jnp.float32)
    mixed = lax.psum(partial_value.astype(jnp.bfloat16), "mp").astype(jnp.float32)
    out_full = (wide + gate_row * mixed).astype(jnp.bfloat16)
    out_local = lax.dynamic_slice_in_dim(out_full, mp_offset, shard_width, 1)
    other_full = passed_along(out_full, "side", 1)
    differ = out_full.astype(jnp.float32) - other_full.astype(jnp.float32)
    grad_out = (gate_row * differ * valid_col / jnp.sqrt(valid_total)).astype(jnp.bfloat16)

    def backprop():
        grad_act = lax.dot_general(
            grad_out, down_full, (((1,), (1,)), ((), ())), preferred_element_type=jnp.float32
        )
        unused, pullback = jax.vjp(gelu_tanh, hidden_pre)
        return pullback(grad_act)[0].astype(jnp.bfloat16)

    def no_backprop():
        return jnp.zeros(hidden_pre.shape, jnp.bfloat16)

    grad_pre = lax.cond(is_student, backprop, no_backprop)
    ff_width = hidden_act.shape[1]

    def product():
        return lax.dot_general(
            normed, grad_pre, (((0,), (0,)), ((), ())), preferred_element_type=jnp.float32
        )

    def nothing():
        return jnp.zeros(
            (width // lax.axis_size(("dp", "side")) * lax.axis_size(("dp", "side")), ff_width),
            jnp.float32,
        )

    up_share = lax.psum_scatter(
        lax.cond(is_student, product, nothing).astype(jnp.bfloat16),
        ("dp", "side"),
        scatter_dimension=0,
        tiled=True,
    ).astype(jnp.float32)

    def down_product():
        return lax.dot_general(
            hidden_act, grad_out, (((0,), (0,)), ((), ())), preferred_element_type=jnp.float32
        )

    def down_nothing():
        return jnp.zeros((ff_width, width), jnp.float32)

    down_term = lax.cond(is_student, down_product, down_nothing)
    down_share = lax.psum_scatter(
        down_term.astype(jnp.bfloat16), ("dp", "side"), scatter_dimension=1, tiled=True
    ).astype(jnp.float32)
    return (out_local[None], up_share, down_share)


def solution(mesh):
    placed = (
        P("dp", "mp"),
        P("side", "dp", "mp"),
        P("side", "mp", "dp"),
        P("side", None, None, None),
        P("dp"),
        P(),
    )
    return jax.shard_map(
        shards,
        mesh=mesh,
        in_specs=placed,
        out_specs=(P("side", "dp", "mp"), P(("dp", "side"), "mp"), P("mp", ("dp", "side"))),
        check_vma=False,
    )
```

profile of v0, /device:TPU:1, one launch (start us, length us, event | category | flops | bytes accessed | tf_op | source)
XLA Modules:
  0.0 593.4 jit_solution(2284106600337096998)
XLA Ops:
  9.4 6.5 %reduce = f32[50,3,3072]{2,1,0:T(4,128)S(1)} reduce(f32[1,50,3,3072]{3,0,2,1:T(1,128)} %param.15, f32[]{:T(128)} %constant.65), dimensions={0}, to_apply=%param.15.reduce_sub_computation | reduce | bytes 3686404 | tf_op args[3]
  16.5 1.2 copy.14
  19.1 29.2 %all-gather.6.cloned.1.call-done = bf16[256,3072]{1,0:T(8,128)(2,1)} async-done(((bf16[256,384]{1,0:T(8,128)(2,1)}), bf16[256,3072]{1,0:T(8,128)(2,1)}) %all-gather.6.cloned.1.call-update) | async-done | bytes 1572880 | tf_op jit(solution)/shard_map/all_gather | solution.py:18
  48.2 1.8 convert_reduce_fusion
  50.1 2.0 fusion.11
  52.8 41.7 %all-gather.8.cloned.1.call-done = bf16[1,3072,768]{2,1,0:T(8,128)(2,1)} async-done(((bf16[1,192,768]{2,1,0:T(8,128)(2,1)}), bf16[1,3072,768]{2,1,0:T(8,128)(2,1)}) %all-gather.8.cloned.1.call-update) | async-done | bytes 4718608 | tf_op jit(solution)/shard_map/all_gather | solution.py:40
  94.5 4.6 fusion.23
  99.2 37.7 %all-gather.10.cloned.1.call-done = bf16[1,768,3072]{1,2,0:T(8,128)(2,1)} async-done(((bf16[1,768,192]{1,2,0:T(8,128)(2,1)}), bf16[1,768,3072]{1,2,0:T(8,128)(2,1)}) %all-gather.10.cloned.1.call-update) | async-done | bytes 4718608 | tf_op jit(solution)/shard_map/all_gather | solution.py:44
  136.9 4.9 convolution_convert_fusion
  142.1 74.3 %all-reduce.2.cloned.1.call-done = bf16[256,3072]{1,0:T(8,128)(2,1)} async-done(((bf16[256,3072]{1,0:T(8,128)(2,1)}), bf16[256,3072]{1,0:T(8,128)(2,1)}) %all-reduce.2.cloned.1.call-update) | async-done | bytes 1572880 | tf_op jit(solution)/shard_map/psum | solution.py:50
  216.3 3.1 fusion.15
  219.5 5.8 collective-permute-start
  227.8 25.6 %collective-permute-done = bf16[256,3072]{1,0:T(8,128)(2,1)} collective-permute-done((bf16[256,3072]{1,0:T(8,128)(2,1)}, bf16[256,3072]{1,0:T(8,128)(2,1)}, u32[]{:S(2)}, u32[]{:S(2)}) %collective-permute-start) | collective-permute-done | bytes 1572896 | tf_op jit(solution)/shard_map/ppermute | solution.py:10
  253.4 2.6 divide_convert_fusion
  256.1 2.5 conditional.4
  256.1 2.5 broadcast.75
  259.6 2.8 conditional.5
  259.6 2.8 broadcast.76
  262.4 6.6 %copy.12 = bf16[768,3072]{0,1:T(8,128)(2,1)} copy(bf16[768,3072]{1,0:T(8,128)(2,1)} %get-tuple-element.43) | data formatting | bytes 9437184 | tf_op jit(solution)/shard_map/cond | solution.py:96
  269.0 1.6 dynamic-slice_bitcast_fusion
  270.6 155.2 %reduce-scatter.3.cloned.1.call-done = bf16[96,768]{1,0:T(8,128)(2,1)} async-done(((bf16[3072,768]{1,0:T(8,128)(2,1)}), bf16[96,768]{1,0:T(8,128)(2,1)}) %reduce-scatter.3.cloned.1.call-update) | async-done | bytes 147472 | tf_op jit(solution)/shard_map/reduce_scatter | solution.py:81
  425.9 1.6 convert_element_type.71
  427.5 157.4 %reduce-scatter.5.cloned.1.call-done = bf16[768,96]{0,1:T(8,128)(2,1)} async-done(((bf16[768,3072]{0,1:T(8,128)(2,1)}), bf16[768,96]{0,1:T(8,128)(2,1)}) %reduce-scatter.5.cloned.1.call-update) | async-done | bytes 147472 | tf_op jit(solution)/shard_map/reduce_scatter | solution.py:97
  584.9 1.6 convert_element_type.73
  (31 shorter events, 7.5 us)
Async XLA Ops:
  7.2 41.1 %all-gather.6.cloned.1.call-start = ((), (), s32[]{:S(2)}) async-start(), calls=%async_computation.2 | async-start | bytes 1769472 | tf_op jit(solution)/shard_map/all_gather | solution.py:18
  7.9 86.6 %all-gather.8.cloned.1.call-start = ((), (), s32[]{:S(2)}) async-start(), calls=%async_computation.6 | async-start | bytes 5013504 | tf_op jit(solution)/shard_map/all_gather | solution.py:40
  8.6 128.2 %all-gather.10.cloned.1.call-start = ((), (), s32[]{:S(2)}) async-start(), calls=%async_computation.7 | async-start | bytes 5013504 | tf_op jit(solution)/shard_map/all_gather | solution.py:44
  9.4 207.0 %all-reduce.2.cloned.1.call-start = ((), (), s32[]{:S(2)}) async-start(), calls=%async_computation.3 | async-start | bytes 3145728 | tf_op jit(solution)/shard_map/psum | solution.py:50
  48.2 3.8 copy-start
  99.2 42.7 %copy-start.1 = (bf16[256,768]{1,0:T(8,128)(2,1)}, bf16[256,768]{1,0:T(8,128)(2,1)S(1)}, u32[]{:S(2)}) copy-start(bf16[256,768]{1,0:T(8,128)(2,1)S(1)} %get-tuple-element.39) | copy-start | bytes 1179652
  141.8 83.4 %copy-start.3 = (s32[16]{0:T(128)S(1)}, s32[16]{0:T(128)}, u32[]{:S(2)}) copy-start(s32[16]{0:T(128)} %param.17) | copy-start | bytes 196
  141.8 284.0 %reduce-scatter.3.cloned.1.call-start = ((), (), s32[]{:S(2)}) async-start(), calls=%async_computation.4 | async-start | bytes 4866048 | tf_op jit(solution)/shard_map/reduce_scatter | solution.py:81
  219.5 34.0 %collective-permute-start = (bf16[256,3072]{1,0:T(8,128)(2,1)}, bf16[256,3072]{1,0:T(8,128)(2,1)}, u32[]{:S(2)}, u32[]{:S(2)}) collective-permute-start(bf16[256,3072]{1,0:T(8,128)(2,1)} %fusion.15), channel_id=1, source_target_pairs={{0,1},{2,3},{4,5},{6,7},{8,9},{10,11},{12,13},{14,15},{16,17},{18,... | collective-permute-start | bytes 4718600 | tf_op jit(solution)/shard_map/ppermute | solution.py:10
  258.6 1.0 copy-start.2
  258.6 326.3 %reduce-scatter.5.cloned.1.call-start = ((), (), s32[]{:S(2)}) async-start(), calls=%async_computation.5 | async-start | bytes 4866048 | tf_op jit(solution)/shard_map/reduce_scatter | solution.py:97
Sparse Core Ops, SparseCore 0:
  9.8 38.4 all-gather.5
  50.1 44.3 all-gather.7
  96.4 40.4 all-gather.9
  142.0 74.3 all-reduce.1
  258.7 167.0 reduce-scatter.2
  428.2 156.6 reduce-scatter.4
where the time goes:
time: 594 us; the launch traced here: 593 us
  waiting for transfers between devices  523 us (88%)
  other arithmetic  21.3 us (4%)
  local copies, waits for them, and re-layouts  16.8 us (3%)
  between operations  15.5 us (3%)
  matrix products  10.3 us (2%)
  starting transfers between devices  6.19 us (1%)
    reduce_scatter x1, waiting for transfers between devices, shards(): lax.psum_scatter(down_term.astype(jnp.bfloat16), ('dp', 'side'), scatter_...  157 us
    reduce_scatter x1, waiting for transfers between devices, shards(): lax.psum_scatter(lax.cond(is_student, product, nothing).astype(jnp.bfloat...  155 us
    psum x1, waiting for transfers between devices, shards(): lax.psum(partial_value.astype(jnp.bfloat16), 'mp').astype(jnp.float32)  74.3 us
    all_gather x1, waiting for transfers between devices, shards(): lax.all_gather(up_weight[0], 'dp', axis=0, tiled=True)  41.7 us
    all_gather x1, waiting for transfers between devices, shards(): down_full = lax.all_gather(down_weight[0], 'dp', axis=1, tiled=True)  37.7 us
    all_gather x1, waiting for transfers between devices, shards(): gathered = lax.all_gather(tokens, 'mp', axis=1, tiled=True)  29.2 us
    ppermute x1, waiting for transfers between devices, passed_along(): return lax.ppermute(x, axis, pairs)  25.6 us
  transfers between devices with their start and end apart: 7, of which 7 were waited for; matrix products, arithmetic and copies ran while one was open for 6% of the time, Pallas kernels for 0%

commit v1 on v0

--- a/solution.py
+++ b/solution.py
@@ -41,7 +41,7 @@
         preferred_element_type=jnp.float32,
     )
     hidden_act = gelu_tanh(hidden_pre).astype(jnp.bfloat16)
-    down_full = lax.all_gather(down_weight[0], "dp", axis=1, tiled=True)
+    down_full = jnp.concatenate(lax.all_gather(down_weight[0], "dp"), axis=1)
     partial_value = jnp.dot(hidden_act, down_full, preferred_element_type=jnp.float32)
     positions = jnp.arange(normed.shape[0], dtype=jnp.int32)
     own_count = lax.dynamic_index_in_dim(valid_counts, lax.axis_index("dp"), 0, keepdims=False)

time: 594 us -> 594 us (level)
  no operation moved by 1% of the time
where the time goes in v1:
time: 594 us; the launch traced here: 593 us
  waiting for transfers between devices  523 us (88%)
  other arithmetic  21.3 us (4%)
  local copies, waits for them, and re-layouts  16.8 us (3%)
  between operations  15.5 us (3%)
  matrix products  10.3 us (2%)
  starting transfers between devices  6.19 us (1%)
    reduce_scatter x1, waiting for transfers between devices, shards(): lax.psum_scatter(down_term.astype(jnp.bfloat16), ('dp', 'side'), scatter_...  157 us
    reduce_scatter x1, waiting for transfers between devices, shards(): lax.psum_scatter(lax.cond(is_student, product, nothing).astype(jnp.bfloat...  155 us
    psum x1, waiting for transfers between devices, shards(): lax.psum(partial_value.astype(jnp.bfloat16), 'mp').astype(jnp.float32)  74.3 us
    all_gather x1, waiting for transfers between devices, shards(): lax.all_gather(up_weight[0], 'dp', axis=0, tiled=True)  41.7 us
    all_gather x1, waiting for transfers between devices, shards(): down_full = jnp.concatenate(lax.all_gather(down_weight[0], 'dp'), axis=1)  37.7 us
    all_gather x1, waiting for transfers between devices, shards(): gathered = lax.all_gather(tokens, 'mp', axis=1, tiled=True)  29.2 us
    ppermute x1, waiting for transfers between devices, passed_along(): return lax.ppermute(x, axis, pairs)  25.6 us
  transfers between devices with their start and end apart: 7, of which 7 were waited for; matrix products, arithmetic and copies ran while one was open for 6% of the time, Pallas kernels for 0%

profile of v1, /device:TPU:1, one launch (start us, length us, event | category | flops | bytes accessed | tf_op | source)
XLA Modules:
  0.0 593.4 jit_solution(2284106600337096998)
XLA Ops:
  9.4 6.5 %reduce = f32[50,3,3072]{2,1,0:T(4,128)S(1)} reduce(f32[1,50,3,3072]{3,0,2,1:T(1,128)} %param.15, f32[]{:T(128)} %constant.65), dimensions={0}, to_apply=%param.15.reduce_sub_computation | reduce | bytes 3686404 | tf_op args[3]
  16.5 1.2 copy.16
  19.1 29.2 %all-gather.5.cloned.1.call-done = bf16[256,3072]{1,0:T(8,128)(2,1)} async-done(((bf16[256,384]{1,0:T(8,128)(2,1)}), bf16[256,3072]{1,0:T(8,128)(2,1)}) %all-gather.5.cloned.1.call-update) | async-done | bytes 1572880 | tf_op jit(solution)/shard_map/all_gather | solution.py:18
  48.2 1.8 convert_reduce_fusion
  50.1 2.0 fusion.11
  52.8 41.7 %all-gather.9.cloned.1.call-done = bf16[1,3072,768]{2,1,0:T(8,128)(2,1)} async-done(((bf16[1,192,768]{2,1,0:T(8,128)(2,1)}), bf16[1,3072,768]{2,1,0:T(8,128)(2,1)}) %all-gather.9.cloned.1.call-update) | async-done | bytes 4718608 | tf_op jit(solution)/shard_map/all_gather | solution.py:40
  94.5 4.6 fusion.23
  99.2 37.7 %all-gather.7.cloned.1.call-done = bf16[16,768,192]{1,2,0:T(8,128)(2,1)} async-done(((bf16[1,768,192]{1,2,0:T(8,128)(2,1)}), bf16[16,768,192]{1,2,0:T(8,128)(2,1)}) %all-gather.7.cloned.1.call-update) | async-done | bytes 4718608 | tf_op jit(solution)/shard_map/all_gather | solution.py:44
  136.9 4.9 convolution_convert_fusion
  142.1 74.3 %all-reduce.2.cloned.1.call-done = bf16[256,3072]{1,0:T(8,128)(2,1)} async-done(((bf16[256,3072]{1,0:T(8,128)(2,1)}), bf16[256,3072]{1,0:T(8,128)(2,1)}) %all-reduce.2.cloned.1.call-update) | async-done | bytes 1572880 | tf_op jit(solution)/shard_map/psum | solution.py:50
  216.3 3.1 fusion.15
  219.5 5.8 collective-permute-start
  227.8 25.6 %collective-permute-done = bf16[256,3072]{1,0:T(8,128)(2,1)} collective-permute-done((bf16[256,3072]{1,0:T(8,128)(2,1)}, bf16[256,3072]{1,0:T(8,128)(2,1)}, u32[]{:S(2)}, u32[]{:S(2)}) %collective-permute-start) | collective-permute-done | bytes 1572896 | tf_op jit(solution)/shard_map/ppermute | solution.py:10
  253.4 2.6 divide_convert_fusion
  256.1 2.5 conditional.4
  256.1 2.5 broadcast.75
  259.6 2.8 conditional.5
  259.6 2.8 broadcast.76
  262.4 6.6 %copy.14 = bf16[768,3072]{0,1:T(8,128)(2,1)} copy(bf16[768,3072]{1,0:T(8,128)(2,1)} %get-tuple-element.46) | data formatting | bytes 9437184 | tf_op jit(solution)/shard_map/cond | solution.py:96
  269.0 1.6 dynamic-slice_bitcast_fusion
  270.6 155.2 %reduce-scatter.3.cloned.1.call-done = bf16[96,768]{1,0:T(8,128)(2,1)} async-done(((bf16[3072,768]{1,0:T(8,128)(2,1)}), bf16[96,768]{1,0:T(8,128)(2,1)}) %reduce-scatter.3.cloned.1.call-update) | async-done | bytes 147472 | tf_op jit(solution)/shard_map/reduce_scatter | solution.py:81
  425.9 1.6 convert_element_type.71
  427.5 157.4 %reduce-scatter.5.cloned.1.call-done = bf16[768,96]{0,1:T(8,128)(2,1)} async-done(((bf16[768,3072]{0,1:T(8,128)(2,1)}), bf16[768,96]{0,1:T(8,128)(2,1)}) %reduce-scatter.5.cloned.1.call-update) | async-done | bytes 147472 | tf_op jit(solution)/shard_map/reduce_scatter | solution.py:97
  584.9 1.6 convert_element_type.73
  (31 shorter events, 7.5 us)
Async XLA Ops:
  7.2 41.1 %all-gather.5.cloned.1.call-start = ((), (), s32[]{:S(2)}) async-start(), calls=%async_computation.2 | async-start | bytes 1769472 | tf_op jit(solution)/shard_map/all_gather | solution.py:18
  7.9 86.6 %all-gather.9.cloned.1.call-start = ((), (), s32[]{:S(2)}) async-start(), calls=%async_computation.7 | async-start | bytes 5013504 | tf_op jit(solution)/shard_map/all_gather | solution.py:40
  8.6 128.2 %all-gather.7.cloned.1.call-start = ((), (), s32[]{:S(2)}) async-start(), calls=%async_computation.3 | async-start | bytes 5013504 | tf_op jit(solution)/shard_map/all_gather | solution.py:44
  9.4 207.0 %all-reduce.2.cloned.1.call-start = ((), (), s32[]{:S(2)}) async-start(), calls=%async_computation.4 | async-start | bytes 3145728 | tf_op jit(solution)/shard_map/psum | solution.py:50
  48.2 3.8 copy-start
  99.2 42.7 %copy-start.1 = (bf16[256,768]{1,0:T(8,128)(2,1)}, bf16[256,768]{1,0:T(8,128)(2,1)S(1)}, u32[]{:S(2)}) copy-start(bf16[256,768]{1,0:T(8,128)(2,1)S(1)} %get-tuple-element.42) | copy-start | bytes 1179652
  141.8 83.4 %copy-start.3 = (s32[16]{0:T(128)S(1)}, s32[16]{0:T(128)}, u32[]{:S(2)}) copy-start(s32[16]{0:T(128)} %param.17) | copy-start | bytes 196
  141.8 284.0 %reduce-scatter.3.cloned.1.call-start = ((), (), s32[]{:S(2)}) async-start(), calls=%async_computation.5 | async-start | bytes 4866048 | tf_op jit(solution)/shard_map/reduce_scatter | solution.py:81
  219.5 34.0 %collective-permute-start = (bf16[256,3072]{1,0:T(8,128)(2,1)}, bf16[256,3072]{1,0:T(8,128)(2,1)}, u32[]{:S(2)}, u32[]{:S(2)}) collective-permute-start(bf16[256,3072]{1,0:T(8,128)(2,1)} %fusion.15), channel_id=1, source_target_pairs={{0,1},{2,3},{4,5},{6,7},{8,9},{10,11},{12,13},{14,15},{16,17},{18,... | collective-permute-start | bytes 4718600 | tf_op jit(solution)/shard_map/ppermute | solution.py:10
  258.6 1.0 copy-start.2
  258.6 326.3 %reduce-scatter.5.cloned.1.call-start = ((), (), s32[]{:S(2)}) async-start(), calls=%async_computation.6 | async-start | bytes 4866048 | tf_op jit(solution)/shard_map/reduce_scatter | solution.py:97
Sparse Core Ops, SparseCore 0:
  9.8 38.4 all-gather.4
  50.1 44.3 all-gather.8
  96.4 40.4 all-gather.6
  142.0 74.3 all-reduce.1
  258.7 167.0 reduce-scatter.2
  428.2 156.6 reduce-scatter.4
